TPU v7x, 256 devices: a whole 4x4x8 slice. The times are simulated.
256 devices in a mesh: dp: 16 (over z, y_lo), dep: 4 (over x), hgt: 4 (over y_hi, core).
Axes of the slice: x: 4, y: 4 (y_hi: 2, y_lo: 2; y = y_hi * 2 + y_lo), z: 8, core: 2. Of those that a mesh axis runs over, the one named last changes fastest.
Arguments:
- volume: bfloat16 [16, 32, 8, 32, 128], P('dp', None, 'dep', 'hgt'), may hold values from -6 to 6
- kernel_first: bfloat16 [27, 64, 32], replicated, may hold values from -0.21875 to 0.21875
- kernel_second: bfloat16 [27, 128, 64], replicated, may hold values from -0.15625 to 0.15625
- cotangent: bfloat16 [16, 128, 8, 32, 128], P('dp', None, 'dep', 'hgt'), may hold values from -0.01171875 to 0.01171875
Outputs:
- features: bfloat16 [16, 128, 8, 32, 128], P('dp', None, 'dep', 'hgt')
- grad_first: float32 [27, 64, 32], P(None, 'dp')
- grad_second: float32 [27, 128, 64], P(None, 'dp')
All inputs are finite; a program needn't handle non-finite values.
Results may differ from a plain program's by a relative error of at most 0.0049.
Values may be sent and summed in bfloat16 or wider, within the bound.
A program may use at most 64 MiB of HBM per device.

v0:
```python
import jax
import jax.numpy as jnp
from jax import lax
from jax.sharding import PartitionSpec as P

OFFSETS = [
    (first, second, third) for first in (-1, 0, 1) for second in (-1, 0, 1) for third in (-1, 0, 1)
]


def extended_2(x, sides, width):
    for axis, dim in sides:
        size, length = (lax.axis_size(axis), x.shape[dim])
        up = [(i, (i + 1) % size) for i in range(size - 1)]
        down = [(j, i) for i, j in up]
        last = lax.slice_in_dim(x, length - width, length, axis=dim)
        leading = lax.slice_in_dim(x, 0, width, axis=dim)
        before = lax.ppermute(last, axis, up)
        after = lax.ppermute(leading, axis, down)
        x = jnp.concatenate([before, x, after], axis=dim)
    return x


def widen(field):
    return jnp.pad(field, ((0, 0), (0, 0), (0, 0), (0, 0), (1, 1)))


def window(padded, shift_d, shift_h, shift_w, depth, height, width):
    return padded[
        :,
        :,
        1 + shift_d : 1 + shift_d + depth,
        1 + shift_h : 1 + shift_h + height,
        1 + shift_w : 1 + shift_w + width,
    ]


def convolve(extended, kernel, depth, height, width):
    padded = widen(extended)
    total = None
    for number, shift in enumerate(OFFSETS):
        piece = window(padded, shift[0], shift[1], shift[2], depth, height, width)
        term = jnp.einsum(
            "oi,bidhw->bodhw", kernel[number], piece, preferred_element_type=jnp.float32
        )
        total = term if total is None else total + term
    return total


def kernel_grad(upstream, extended, depth, height, width):
    padded = widen(extended)
    parts = []
    for shift in OFFSETS:
        piece = window(padded, shift[0], shift[1], shift[2], depth, height, width)
        parts.append(
            jnp.einsum("bodhw,bidhw->oi", upstream, piece, preferred_element_type=jnp.float32)
        )
    return jnp.stack(parts)


def per_device(volume, kernel_first, kernel_second, cotangent):
    depth, height, width = (volume.shape[2], volume.shape[3], volume.shape[4])
    vol_rim = extended_2(volume, (("dep", 2), ("hgt", 3)), 1)
    pre = convolve(vol_rim, kernel_first, depth, height, width)
    hidden = jax.nn.silu(pre).astype(jnp.bfloat16)
    hidden_rim = extended_2(hidden, (("dep", 2), ("hgt", 3)), 1)
    features = convolve(hidden_rim, kernel_second, depth, height, width).astype(jnp.bfloat16)
    cot_rim = extended_2(cotangent, (("dep", 2), ("hgt", 3)), 1)
    grad_second = kernel_grad(cotangent, hidden_rim, depth, height, width)
    padded_cot = widen(cot_rim)
    back = None
    for number, shift in enumerate(OFFSETS):
        piece = window(padded_cot, -shift[0], -shift[1], -shift[2], depth, height, width)
        term = jnp.einsum(
            "oi,bodhw->bidhw", kernel_second[number], piece, preferred_element_type=jnp.float32
        )
        back = term if back is None else back + term
    sigma = jax.nn.sigmoid(pre)
    delta = (back * (sigma * (1.0 + pre * (1.0 - sigma)))).astype(jnp.bfloat16)
    grad_first = kernel_grad(delta, vol_rim, depth, height, width)
    summed = lax.psum((grad_first, grad_second), ("dep", "hgt"))
    grad_first, grad_second = (
        lax.psum_scatter(summed[0], "dp", scatter_dimension=1, tiled=True),
        lax.psum_scatter(summed[1], "dp", scatter_dimension=1, tiled=True),
    )
    return (features, grad_first, grad_second)


def solution(mesh):
    placed = (P("dp", None, "dep", "hgt", None), P(), P(), P("dp", None, "dep", "hgt", None))
    return jax.shard_map(
        per_device,
        mesh=mesh,
        in_specs=placed,
        out_specs=(P("dp", None, "dep", "hgt", None), P(None, "dp", None), P(None, "dp", None)),
        check_vma=False,
    )
```

profile of v0, /device:TPU:8, one launch (start us, length us, event | category | flops | bytes accessed | tf_op | source)
XLA Modules:
  0.0 418.0 jit_solution(17139515704096667886)
XLA Ops:
  7.2 0.9 copy.50
  8.2 3.5 collective-permute-start
  11.7 1.4 collective-permute-start.1
  13.2 1.2 copy.56
  14.4 4.6 %collective-permute-start.8 = (bf16[1,128,1,8,128]{4,1,3,2,0:T(8,128)(2,1)S(1)}, bf16[1,128,1,8,128]{4,1,3,2,0:T(8,128)(2,1)S(1)}, u32[]{:S(2)}, u32[]{:S(2)}) collective-permute-start(bf16[1,128,1,8,128]{4,1,3,2,0:T(8,128)(2,1)S(1)} %get-tuple-element.14), channel_id=1, source_target_pairs={{0,4},{4,8},{8,12},{1,5},{5,9},{9,13},{2,6},{6,10},{10,14},{3,7},{... | collective-permute-start | bytes 786440 | tf_op jit(solution)/shard_map/ppermute | solution.py:18
  19.0 1.3 collective-permute-start.9
  20.4 1.3 collective-permute-start.2
  21.7 1.3 collective-permute-start.3
  23.3 4.0 collective-permute-done.3
  35.5 4.6 %collective-permute-start.4 = (bf16[1,64,1,8,128]{4,1,3,2,0:T(8,128)(2,1)S(1)}, bf16[1,64,1,8,128]{4,1,3,2,0:T(8,128)(2,1)S(1)}, u32[]{:S(2)}, u32[]{:S(2)}) collective-permute-start(bf16[1,64,1,8,128]{4,1,3,2,0:T(8,128)(2,1)S(1)} %get-tuple-element.19), channel_id=1, source_target_pairs={{0,4},{4,8},{8,12},{1,5},{5,9},{9,13},{2,6},{6,10},{10,14},{3,7},{... | collective-permute-start | bytes 393224 | tf_op jit(solution)/shard_map/ppermute | solution.py:18
  40.1 1.3 collective-permute-start.5
  41.6 0.9 collective-permute-done.4
  42.6 4.4 %collective-permute-done.5 = bf16[1,64,1,8,128]{4,1,3,2,0:T(8,128)(2,1)S(1)} collective-permute-done((bf16[1,64,1,8,128]{4,1,3,2,0:T(8,128)(2,1)S(1)}, bf16[1,64,1,8,128]{4,1,3,2,0:T(8,128)(2,1)S(1)}, u32[]{:S(2)}, u32[]{:S(2)}) %collective-permute-start.5) | collective-permute-done | bytes 131104 | tf_op jit(solution)/shard_map/ppermute | solution.py:19
  47.0 4.6 %collective-permute-start.6 = (bf16[1,64,4,1,128]{4,1,3,2,0:T(8,128)(2,1)S(1)}, bf16[1,64,4,1,128]{4,1,3,2,0:T(8,128)(2,1)S(1)}, u32[]{:S(2)}, u32[]{:S(2)}) collective-permute-start(bf16[1,64,4,1,128]{4,1,3,2,0:T(8,128)(2,1)S(1)} %get-tuple-element.17), channel_id=1, source_target_pairs={{0,1},{1,2},{2,3},{4,5},{5,6},{6,7},{8,9},{9,10},{10,11},{12,13},{... | collective-permute-start | bytes 196616 | tf_op jit(solution)/shard_map/ppermute | solution.py:18
  51.6 1.3 collective-permute-start.7
  53.5 4.0 collective-permute-start.10
  57.5 1.5 collective-permute-start.11
  60.0 0.9 fusion.85
  61.7 1.5 convolution_bitcast_fusion
  63.3 1.3 convolution_bitcast_fusion.7
  64.7 0.9 fusion.84
  65.6 1.0 fusion.83
  68.4 0.9 fusion.80
  69.3 0.9 fusion.79
  70.3 1.3 convolution_bitcast_fusion.1
  72.5 1.0 fusion.77
  74.4 0.9 fusion.75
  75.3 0.9 fusion.74
  76.2 0.9 fusion.73
  77.2 0.9 fusion.72
  78.1 0.9 fusion.71
  79.0 0.9 fusion.70
  80.8 0.9 fusion.68
  81.8 0.9 fusion.67
  83.6 0.9 fusion.65
  85.5 0.9 fusion.63
  86.4 1.0 fusion.62
  87.3 0.9 fusion.61
  88.3 0.9 fusion.60
  89.2 0.9 fusion.59
  92.3 1.5 convolution_add_fusion.7
  93.8 1.3 convolution_bitcast_fusion.2
  95.1 1.4 convolution_bitcast_fusion.3
  96.6 1.7 fusion.5
  111.9 1.8 copy.63
  113.8 2.1 convolution_bitcast_fusion.5
  115.9 4.0 copy.91
  120.0 2.3 convolution_bitcast_fusion.6
  122.3 2.1 convolution_add_fusion.6
  124.7 2.1 convolution_bitcast_fusion.8
  126.8 2.2 convolution_bitcast_fusion.9
  129.0 1.3 convolution_add_fusion.5
  130.3 1.2 convolution_add_fusion.4
  131.5 1.1 convolution_add_fusion.3
  132.6 1.1 convolution_add_fusion.2
  133.7 1.2 convolution_add_fusion.1
  134.9 1.1 fusion.7
  135.9 53.8 %reduce-scatter.3.cloned.1.call-done = f32[27,4,32]{2,0,1:T(8,128)} async-done(((f32[27,64,32]{2,0,1:T(8,128)}), f32[27,4,32]{2,0,1:T(8,128)}) %reduce-scatter.3.cloned.1.call-update) | async-done | bytes 13840 | tf_op jit(solution)/shard_map/reduce_scatter | solution.py:83
  189.8 76.9 %reduce-scatter.5.cloned.1.call-done = f32[27,8,64]{2,0,1:T(8,128)} async-done(((f32[27,128,64]{2,0,1:T(8,128)}), f32[27,8,64]{2,0,1:T(8,128)}) %reduce-scatter.5.cloned.1.call-update) | async-done | bytes 55312 | tf_op jit(solution)/shard_map/reduce_scatter | solution.py:84
  266.7 4.5 %fusion.27 = bf16[1,128,2,8,128]{1,4,3,2,0:T(8,128)(2,1)S(1)} fusion(f32[1,128,2,8,128]{1,4,3,2,0:T(8,128)} %convolution_bitcast_fusion, f32[1,128,2,8,128]{1,4,3,2,0:T(8,128)} %convolution_bitcast_fusion.1, f32[1,128,2,8,128]{1,4,3,2,0:T(8,128)} %convolution_bitcast_fusion.2, f32[1,128,2,8,128]{1,4,3,2,0:T(8,128)} %convolution_bitcast_fusion.3, ...), kind=kOutput, calls=%fused_computation.64 | convolution fusion | flops 36700160 | bytes 12337152 | tf_op jit(solution)/shard_map/oi,bidhw->bodhw/dot_general | solution.py:43
  271.2 1.2 copy.92
  272.4 136.0 %all-reduce.6.cloned.1.call-done = (f32[27,4,32]{2,0,1:T(8,128)}, f32[27,8,64]{2,0,1:T(8,128)}) async-done(((f32[27,4,32]{2,0,1:T(8,128)}, f32[27,8,64]{2,0,1:T(8,128)}), (f32[27,4,32]{2,0,1:T(8,128)}, f32[27,8,64]{2,0,1:T(8,128)})) %all-reduce.6.cloned.1.call-update) | async-done | bytes 69136 | tf_op jit(solution)/shard_map/psum | solution.py:81
  408.4 1.6 copy.94
  410.0 1.5 copy.93
  (143 shorter events, 33.7 us)
Async XLA Ops:
  7.2 182.6 %reduce-scatter.3.cloned.1.call-start = ((), (), s32[]{:S(2)}) async-start(), calls=%async_computation.2 | async-start | bytes 1114112 | tf_op jit(solution)/shard_map/reduce_scatter | solution.py:83
  8.2 12.1 %copy-start.5 = (bf16[1,32,2,8,128]{4,3,2,1,0:T(8,128)(2,1)S(1)}, bf16[1,32,2,8,128]{4,3,2,1,0:T(8,128)(2,1)}, u32[]{:S(2)}) copy-start(bf16[1,32,2,8,128]{4,3,2,1,0:T(8,128)(2,1)} %param.4) | copy-start | bytes 393220
  8.2 12.1 %collective-permute-start = (bf16[1,32,1,8,128]{4,1,3,2,0:T(8,128)(2,1)S(1)}, bf16[1,32,1,8,128]{4,1,3,2,0:T(8,128)(2,1)S(1)}, u32[]{:S(2)}, u32[]{:S(2)}) collective-permute-start(bf16[1,32,1,8,128]{4,1,3,2,0:T(8,128)(2,1)S(1)} %get-tuple-element.24), channel_id=1, source_target_pairs={{0,4},{4,8},{8,12},{1,5},{5,9},{9,13},{2,6},{6,10},{10,14},{3,7},{... | collective-permute-start | bytes 196616 | tf_op jit(solution)/shard_map/ppermute | solution.py:18
  11.7 11.3 %copy-start.7 = (bf16[27,64,32]{1,2,0:T(8,128)(2,1)S(1)}, bf16[27,64,32]{1,2,0:T(8,128)(2,1)}, u32[]{:S(2)}) copy-start(bf16[27,64,32]{1,2,0:T(8,128)(2,1)} %param.5) | copy-start | bytes 331780
  11.7 8.6 %collective-permute-start.1 = (bf16[1,32,1,8,128]{4,1,3,2,0:T(8,128)(2,1)S(1)}, bf16[1,32,1,8,128]{4,1,3,2,0:T(8,128)(2,1)S(1)}, u32[]{:S(2)}, u32[]{:S(2)}) collective-permute-start(bf16[1,32,1,8,128]{4,1,3,2,0:T(8,128)(2,1)S(1)} %get-tuple-element.23), channel_id=1, source_target_pairs={{4,0},{8,4},{12,8},{5,1},{9,5},{13,9},{6,2},{10,6},{14,10},{7,3},{... | collective-permute-start | bytes 196616 | tf_op jit(solution)/shard_map/ppermute | solution.py:19
  14.4 38.8 %collective-permute-start.8 = (bf16[1,128,1,8,128]{4,1,3,2,0:T(8,128)(2,1)S(1)}, bf16[1,128,1,8,128]{4,1,3,2,0:T(8,128)(2,1)S(1)}, u32[]{:S(2)}, u32[]{:S(2)}) collective-permute-start(bf16[1,128,1,8,128]{4,1,3,2,0:T(8,128)(2,1)S(1)} %get-tuple-element.14), channel_id=1, source_target_pairs={{0,4},{4,8},{8,12},{1,5},{5,9},{9,13},{2,6},{6,10},{10,14},{3,7},{... | collective-permute-start | bytes 786440 | tf_op jit(solution)/shard_map/ppermute | solution.py:18
  19.0 34.5 %collective-permute-start.9 = (bf16[1,128,1,8,128]{4,1,3,2,0:T(8,128)(2,1)S(1)}, bf16[1,128,1,8,128]{4,1,3,2,0:T(8,128)(2,1)S(1)}, u32[]{:S(2)}, u32[]{:S(2)}) collective-permute-start(bf16[1,128,1,8,128]{4,1,3,2,0:T(8,128)(2,1)S(1)} %get-tuple-element.13), channel_id=1, source_target_pairs={{4,0},{8,4},{12,8},{5,1},{9,5},{13,9},{6,2},{10,6},{14,10},{7,3},{... | collective-permute-start | bytes 786440 | tf_op jit(solution)/shard_map/ppermute | solution.py:19
  20.4 2.9 collective-permute-start.2
  21.7 5.6 %collective-permute-start.3 = (bf16[1,32,4,1,128]{4,1,3,2,0:T(8,128)(2,1)S(1)}, bf16[1,32,4,1,128]{4,1,3,2,0:T(8,128)(2,1)S(1)}, u32[]{:S(2)}, u32[]{:S(2)}) collective-permute-start(bf16[1,32,4,1,128]{4,1,3,2,0:T(8,128)(2,1)S(1)} %get-tuple-element.22), channel_id=1, source_target_pairs={{1,0},{2,1},{3,2},{5,4},{6,5},{7,6},{9,8},{10,9},{11,10},{13,12},{... | collective-permute-start | bytes 98312 | tf_op jit(solution)/shard_map/ppermute | solution.py:19
  34.9 6.5 %copy-start = (bf16[1,128,2,8,128]{4,3,2,1,0:T(8,128)(2,1)S(1)}, bf16[1,128,2,8,128]{4,3,2,1,0:T(8,128)(2,1)}, u32[]{:S(2)}) copy-start(bf16[1,128,2,8,128]{4,3,2,1,0:T(8,128)(2,1)} %param.7) | copy-start | bytes 1572868
  34.9 6.5 %copy-start.6 = (bf16[27,128,64]{1,2,0:T(8,128)(2,1)S(1)}, bf16[27,128,64]{1,2,0:T(8,128)(2,1)}, u32[]{:S(2)}) copy-start(bf16[27,128,64]{1,2,0:T(8,128)(2,1)} %param.6) | copy-start | bytes 1327108
  35.5 7.1 %collective-permute-start.4 = (bf16[1,64,1,8,128]{4,1,3,2,0:T(8,128)(2,1)S(1)}, bf16[1,64,1,8,128]{4,1,3,2,0:T(8,128)(2,1)S(1)}, u32[]{:S(2)}, u32[]{:S(2)}) collective-permute-start(bf16[1,64,1,8,128]{4,1,3,2,0:T(8,128)(2,1)S(1)} %get-tuple-element.19), channel_id=1, source_target_pairs={{0,4},{4,8},{8,12},{1,5},{5,9},{9,13},{2,6},{6,10},{10,14},{3,7},{... | collective-permute-start | bytes 393224 | tf_op jit(solution)/shard_map/ppermute | solution.py:18
  40.1 6.9 %collective-permute-start.5 = (bf16[1,64,1,8,128]{4,1,3,2,0:T(8,128)(2,1)S(1)}, bf16[1,64,1,8,128]{4,1,3,2,0:T(8,128)(2,1)S(1)}, u32[]{:S(2)}, u32[]{:S(2)}) collective-permute-start(bf16[1,64,1,8,128]{4,1,3,2,0:T(8,128)(2,1)S(1)} %get-tuple-element.20), channel_id=1, source_target_pairs={{4,0},{8,4},{12,8},{5,1},{9,5},{13,9},{6,2},{10,6},{14,10},{7,3},{... | collective-permute-start | bytes 393224 | tf_op jit(solution)/shard_map/ppermute | solution.py:19
  47.0 12.2 %collective-permute-start.6 = (bf16[1,64,4,1,128]{4,1,3,2,0:T(8,128)(2,1)S(1)}, bf16[1,64,4,1,128]{4,1,3,2,0:T(8,128)(2,1)S(1)}, u32[]{:S(2)}, u32[]{:S(2)}) collective-permute-start(bf16[1,64,4,1,128]{4,1,3,2,0:T(8,128)(2,1)S(1)} %get-tuple-element.17), channel_id=1, source_target_pairs={{0,1},{1,2},{2,3},{4,5},{5,6},{6,7},{8,9},{9,10},{10,11},{12,13},{... | collective-permute-start | bytes 196616 | tf_op jit(solution)/shard_map/ppermute | solution.py:18
  51.6 7.6 %collective-permute-start.7 = (bf16[1,64,4,1,128]{4,1,3,2,0:T(8,128)(2,1)S(1)}, bf16[1,64,4,1,128]{4,1,3,2,0:T(8,128)(2,1)S(1)}, u32[]{:S(2)}, u32[]{:S(2)}) collective-permute-start(bf16[1,64,4,1,128]{4,1,3,2,0:T(8,128)(2,1)S(1)} %get-tuple-element.18), channel_id=1, source_target_pairs={{1,0},{2,1},{3,2},{5,4},{6,5},{7,6},{9,8},{10,9},{11,10},{13,12},{... | collective-permute-start | bytes 196616 | tf_op jit(solution)/shard_map/ppermute | solution.py:19
  53.5 43.1 %collective-permute-start.10 = (bf16[1,128,4,1,128]{4,1,3,2,0:T(8,128)(2,1)S(1)}, bf16[1,128,4,1,128]{4,1,3,2,0:T(8,128)(2,1)S(1)}, u32[]{:S(2)}, u32[]{:S(2)}) collective-permute-start(bf16[1,128,4,1,128]{4,1,3,2,0:T(8,128)(2,1)S(1)} %get-tuple-element.11), channel_id=1, source_target_pairs={{0,1},{1,2},{2,3},{4,5},{5,6},{6,7},{8,9},{9,10},{10,11},{12,13},{... | collective-permute-start | bytes 393224 | tf_op jit(solution)/shard_map/ppermute | solution.py:18
  57.5 39.1 %collective-permute-start.11 = (bf16[1,128,4,1,128]{4,1,3,2,0:T(8,128)(2,1)S(1)}, bf16[1,128,4,1,128]{4,1,3,2,0:T(8,128)(2,1)S(1)}, u32[]{:S(2)}, u32[]{:S(2)}) collective-permute-start(bf16[1,128,4,1,128]{4,1,3,2,0:T(8,128)(2,1)S(1)} %get-tuple-element.12), channel_id=1, source_target_pairs={{1,0},{2,1},{3,2},{5,4},{6,5},{7,6},{9,8},{10,9},{11,10},{13,12},{... | collective-permute-start | bytes 393224 | tf_op jit(solution)/shard_map/ppermute | solution.py:19
  63.3 26.8 %copy-start.4 = (bf16[1,64,4,9,128]{4,1,3,2,0:T(8,128)(2,1)}, bf16[1,64,4,9,128]{4,1,3,2,0:T(8,128)(2,1)S(1)}, u32[]{:S(2)}) copy-start(bf16[1,64,4,9,128]{4,1,3,2,0:T(8,128)(2,1)S(1)} %get-tuple-element.15) | copy-start | bytes 1769476
  63.3 28.7 %copy-start.3 = (bf16[1,64,4,9,128]{4,1,3,2,0:T(8,128)(2,1)}, bf16[1,64,4,9,128]{4,1,3,2,0:T(8,128)(2,1)S(1)}, u32[]{:S(2)}) copy-start(bf16[1,64,4,9,128]{4,1,3,2,0:T(8,128)(2,1)S(1)} %get-tuple-element.16) | copy-start | bytes 1769476
  113.8 152.9 %reduce-scatter.5.cloned.1.call-start = ((), (), s32[]{:S(2)}) async-start(), calls=%async_computation.3 | async-start | bytes 2228224 | tf_op jit(solution)/shard_map/reduce_scatter | solution.py:84
  120.0 2.3 copy-start.1
  124.4 284.0 %all-reduce.6.cloned.1.call-start = ((), (), s32[]{:S(2)}) async-start(), calls=%async_computation.4 | async-start | bytes 393216 | tf_op jit(solution)/shard_map/psum | solution.py:81
  124.7 4.3 %copy-start.2 = (f32[2,8,128,128]{3,2,1,0:T(8,128)S(1)}, f32[2,8,128,128]{3,2,1,0:T(8,128)}, u32[]{:S(2)}) copy-start(f32[2,8,128,128]{3,2,1,0:T(8,128)} %convolution_add_fusion.6) | copy-start | bytes 3145732
Sparse Core Ops, SparseCore 0:
  113.9 75.8 reduce-scatter.2
  192.5 74.1 reduce-scatter.4
  269.6 138.7 all-reduce.5
where the time goes:
time: 419 us; the launch traced here: 418 us
  waiting for transfers between devices  276 us (66%)
  matrix products  80.8 us (19%)
  starting transfers between devices  31 us (7%)
  between operations  14.5 us (3%)
  local copies, waits for them, and re-layouts  12.7 us (3%)
    psum x1, waiting for transfers between devices, per_device(): summed = lax.psum((grad_first, grad_second), ('dep', 'hgt'))  136 us
    reduce_scatter x1, waiting for transfers between devices, per_device(): lax.psum_scatter(summed[1], 'dp', scatter_dimension=1, tiled=True)  76.9 us
    reduce_scatter x1, waiting for transfers between devices, per_device(): lax.psum_scatter(summed[0], 'dp', scatter_dimension=1, tiled=True)  53.8 us
    dot_general x54, matrix products, convolve(): jnp.einsum('oi,bidhw->bodhw', kernel[number], piece, preferred_element_ty...  41.9 us
    dot_general x54, matrix products, kernel_grad(): jnp.einsum('bodhw,bidhw->oi', upstream, piece, preferred_element_type=jnp...  31.1 us
    ppermute x6, starting transfers between devices, extended_2(): before = lax.ppermute(last, axis, up)  22.5 us
    ppermute x6, waiting for transfers between devices, extended_2(): after = lax.ppermute(leading, axis, down)  8.42 us
  transfers between devices with their start and end apart: 15, of which 6 were waited for; matrix products, arithmetic and copies ran while one was open for 18% of the time, Pallas kernels for 0%

commit v1 on v0

--- a/solution.py
+++ b/solution.py
@@ -78,7 +78,7 @@
     sigma = jax.nn.sigmoid(pre)
     delta = (back * (sigma * (1.0 + pre * (1.0 - sigma)))).astype(jnp.bfloat16)
     grad_first = kernel_grad(delta, vol_rim, depth, height, width)
-    summed = lax.psum((grad_first, grad_second), ("dep", "hgt"))
+    summed = lax.psum(lax.psum((grad_first, grad_second), "hgt"), "dep")
     grad_first, grad_second = (
         lax.psum_scatter(summed[0], "dp", scatter_dimension=1, tiled=True),
         lax.psum_scatter(summed[1], "dp", scatter_dimension=1, tiled=True),

time: 419 us -> 374 us (0.89)
  waiting for transfers between devices: 276 us -> 230 us
    psum x1 -> x2, waiting for transfers between devices: 136 us -> 90.1 us  [per_device(): summed = lax.psum(lax.psum((grad_first, grad_second), 'hgt'), 'dep')]
  transfers between devices with their start and end apart: 15 -> 16, of which waited for: 6 -> 7; matrix products, arithmetic and copies ran while one was open for 18% -> 20% of each run, Pallas kernels for 0% -> 0%
where the time goes in v1:
time: 374 us; the launch traced here: 373 us
  waiting for transfers between devices  230 us (61%)
  matrix products  81.6 us (22%)
  starting transfers between devices  31 us (8%)
  between operations  14.5 us (4%)
  local copies, waits for them, and re-layouts  12.7 us (3%)
    psum x2, waiting for transfers between devices, per_device(): summed = lax.psum(lax.psum((grad_first, grad_second), 'hgt'), 'dep')  90.1 us
    reduce_scatter x1, waiting for transfers between devices, per_device(): lax.psum_scatter(summed[1], 'dp', scatter_dimension=1, tiled=True)  76.8 us
    reduce_scatter x1, waiting for transfers between devices, per_device(): lax.psum_scatter(summed[0], 'dp', scatter_dimension=1, tiled=True)  53.9 us
    dot_general x54, matrix products, convolve(): jnp.einsum('oi,bidhw->bodhw', kernel[number], piece, preferred_element_ty...  42.6 us
    dot_general x54, matrix products, kernel_grad(): jnp.einsum('bodhw,bidhw->oi', upstream, piece, preferred_element_type=jnp...  31.1 us
    ppermute x6, starting transfers between devices, extended_2(): before = lax.ppermute(last, axis, up)  22.5 us
    ppermute x6, waiting for transfers between devices, extended_2(): after = lax.ppermute(leading, axis, down)  8.42 us
    ppermute x6, starting transfers between devices, extended_2(): after = lax.ppermute(leading, axis, down)  8.06 us
  transfers between devices with their start and end apart: 16, of which 7 were waited for; matrix products, arithmetic and copies ran while one was open for 20% of the time, Pallas kernels for 0%

profile of v1, /device:TPU:8, one launch (start us, length us, event | category | flops | bytes accessed | tf_op | source)
XLA Modules:
  0.0 373.0 jit_solution(4920711104044550527)
XLA Ops:
  7.2 0.9 copy.50
  8.2 3.5 collective-permute-start
  11.7 1.4 collective-permute-start.1
  13.2 1.2 copy.56
  14.4 4.6 %collective-permute-start.8 = (bf16[1,128,1,8,128]{4,1,3,2,0:T(8,128)(2,1)S(1)}, bf16[1,128,1,8,128]{4,1,3,2,0:T(8,128)(2,1)S(1)}, u32[]{:S(2)}, u32[]{:S(2)}) collective-permute-start(bf16[1,128,1,8,128]{4,1,3,2,0:T(8,128)(2,1)S(1)} %get-tuple-element.16), channel_id=1, source_target_pairs={{0,4},{4,8},{8,12},{1,5},{5,9},{9,13},{2,6},{6,10},{10,14},{3,7},{... | collective-permute-start | bytes 786440 | tf_op jit(solution)/shard_map/ppermute | solution.py:18
  19.0 1.3 collective-permute-start.9
  20.4 1.3 collective-permute-start.2
  21.7 1.3 collective-permute-start.3
  23.3 4.0 %collective-permute-done.3 = bf16[1,32,4,1,128]{4,1,3,2,0:T(8,128)(2,1)S(1)} collective-permute-done((bf16[1,32,4,1,128]{4,1,3,2,0:T(8,128)(2,1)S(1)}, bf16[1,32,4,1,128]{4,1,3,2,0:T(8,128)(2,1)S(1)}, u32[]{:S(2)}, u32[]{:S(2)}) %collective-permute-start.3) | collective-permute-done | bytes 32800 | tf_op jit(solution)/shard_map/ppermute | solution.py:19
  35.5 4.6 %collective-permute-start.4 = (bf16[1,64,1,8,128]{4,1,3,2,0:T(8,128)(2,1)S(1)}, bf16[1,64,1,8,128]{4,1,3,2,0:T(8,128)(2,1)S(1)}, u32[]{:S(2)}, u32[]{:S(2)}) collective-permute-start(bf16[1,64,1,8,128]{4,1,3,2,0:T(8,128)(2,1)S(1)} %get-tuple-element.21), channel_id=1, source_target_pairs={{0,4},{4,8},{8,12},{1,5},{5,9},{9,13},{2,6},{6,10},{10,14},{3,7},{... | collective-permute-start | bytes 393224 | tf_op jit(solution)/shard_map/ppermute | solution.py:18
  40.1 1.3 collective-permute-start.5
  41.6 0.9 collective-permute-done.4
  42.6 4.4 %collective-permute-done.5 = bf16[1,64,1,8,128]{4,1,3,2,0:T(8,128)(2,1)S(1)} collective-permute-done((bf16[1,64,1,8,128]{4,1,3,2,0:T(8,128)(2,1)S(1)}, bf16[1,64,1,8,128]{4,1,3,2,0:T(8,128)(2,1)S(1)}, u32[]{:S(2)}, u32[]{:S(2)}) %collective-permute-start.5) | collective-permute-done | bytes 131104 | tf_op jit(solution)/shard_map/ppermute | solution.py:19
  47.0 4.6 %collective-permute-start.6 = (bf16[1,64,4,1,128]{4,1,3,2,0:T(8,128)(2,1)S(1)}, bf16[1,64,4,1,128]{4,1,3,2,0:T(8,128)(2,1)S(1)}, u32[]{:S(2)}, u32[]{:S(2)}) collective-permute-start(bf16[1,64,4,1,128]{4,1,3,2,0:T(8,128)(2,1)S(1)} %get-tuple-element.19), channel_id=1, source_target_pairs={{0,1},{1,2},{2,3},{4,5},{5,6},{6,7},{8,9},{9,10},{10,11},{12,13},{... | collective-permute-start | bytes 196616 | tf_op jit(solution)/shard_map/ppermute | solution.py:18
  51.6 1.3 collective-permute-start.7
  53.5 4.0 %collective-permute-start.10 = (bf16[1,128,4,1,128]{4,1,3,2,0:T(8,128)(2,1)S(1)}, bf16[1,128,4,1,128]{4,1,3,2,0:T(8,128)(2,1)S(1)}, u32[]{:S(2)}, u32[]{:S(2)}) collective-permute-start(bf16[1,128,4,1,128]{4,1,3,2,0:T(8,128)(2,1)S(1)} %get-tuple-element.13), channel_id=1, source_target_pairs={{0,1},{1,2},{2,3},{4,5},{5,6},{6,7},{8,9},{9,10},{10,11},{12,13},{... | collective-permute-start | bytes 393224 | tf_op jit(solution)/shard_map/ppermute | solution.py:18
  57.5 1.5 collective-permute-start.11
  60.0 0.9 fusion.85
  61.9 1.3 convolution_bitcast_fusion.7
  64.1 0.9 fusion.83
  66.0 0.9 fusion.81
  66.9 1.0 fusion.80
  68.8 1.3 convolution_bitcast_fusion.1
  70.1 0.9 fusion.78
  71.0 1.0 fusion.77
  73.8 1.0 fusion.74
  74.7 0.9 fusion.73
  75.7 0.9 fusion.72
  76.6 1.0 fusion.71
  77.5 0.9 fusion.70
  78.5 0.9 fusion.69
  79.4 1.0 fusion.68
  81.2 0.9 fusion.66
  82.2 0.9 fusion.65
  83.1 0.9 fusion.64
  84.9 1.0 fusion.62
  85.9 0.9 fusion.61
  87.7 0.9 fusion.59
  90.9 1.5 convolution_add_fusion.7
  92.4 1.5 convolution_bitcast_fusion
  93.9 1.3 convolution_bitcast_fusion.2
  95.2 1.7 fusion.5
  110.6 1.8 copy.63
  112.5 2.2 convolution_bitcast_fusion.3
  114.6 4.0 %copy.91 = f32[27,128,64]{2,0,1:T(8,128)} copy(f32[27,128,64]{1,2,0:T(8,128)} %fusion.59) | data formatting | bytes 1769472 | tf_op jit(solution)/shard_map/stack | solution.py:58
  118.6 2.2 convolution_bitcast_fusion.5
  120.8 2.1 convolution_add_fusion.6
  123.3 2.3 convolution_bitcast_fusion.6
  125.6 2.0 convolution_bitcast_fusion.8
  127.6 1.3 convolution_add_fusion.5
  128.9 1.2 convolution_add_fusion.4
  130.1 1.1 convolution_add_fusion.3
  131.2 1.1 convolution_add_fusion.2
  132.3 1.2 convolution_add_fusion.1
  133.5 1.1 fusion.7
  134.5 53.9 %reduce-scatter.3.cloned.1.call-done = f32[27,4,32]{2,0,1:T(8,128)} async-done(((f32[27,64,32]{2,0,1:T(8,128)}), f32[27,4,32]{2,0,1:T(8,128)}) %reduce-scatter.3.cloned.1.call-update) | async-done | bytes 13840 | tf_op jit(solution)/shard_map/reduce_scatter | solution.py:83
  188.4 76.8 %reduce-scatter.5.cloned.1.call-done = f32[27,8,64]{2,0,1:T(8,128)} async-done(((f32[27,128,64]{2,0,1:T(8,128)}), f32[27,8,64]{2,0,1:T(8,128)}) %reduce-scatter.5.cloned.1.call-update) | async-done | bytes 55312 | tf_op jit(solution)/shard_map/reduce_scatter | solution.py:84
  265.3 2.2 convolution_bitcast_fusion.9
  267.5 46.6 %all-reduce.8.cloned.1.call-done = (f32[27,4,32]{2,0,1:T(8,128)}, f32[27,8,64]{2,0,1:T(8,128)}) async-done(((f32[27,4,32]{2,0,1:T(8,128)}, f32[27,8,64]{2,0,1:T(8,128)}), (f32[27,4,32]{2,0,1:T(8,128)}, f32[27,8,64]{2,0,1:T(8,128)})) %all-reduce.8.cloned.1.call-update) | async-done | bytes 69136 | tf_op jit(solution)/shard_map/psum | solution.py:81
  314.2 4.5 %fusion.27 = bf16[1,128,2,8,128]{1,4,3,2,0:T(8,128)(2,1)S(1)} fusion(f32[1,128,2,8,128]{1,4,3,2,0:T(8,128)} %convolution_bitcast_fusion, f32[1,128,2,8,128]{1,4,3,2,0:T(8,128)} %convolution_bitcast_fusion.1, f32[1,128,2,8,128]{1,4,3,2,0:T(8,128)} %convolution_bitcast_fusion.2, f32[1,128,2,8,128]{1,4,3,2,0:T(8,128)} %convolution_bitcast_fusion.3, ...), kind=kOutput, calls=%fused_computation.64 | convolution fusion | flops 36700160 | bytes 12337152 | tf_op jit(solution)/shard_map/oi,bidhw->bodhw/dot_general | solution.py:43
  318.7 1.2 copy.92
  319.9 43.4 %all-reduce.10.cloned.1.call-done = (f32[27,4,32]{2,0,1:T(8,128)}, f32[27,8,64]{2,0,1:T(8,128)}) async-done(((f32[27,4,32]{2,0,1:T(8,128)}, f32[27,8,64]{2,0,1:T(8,128)}), (f32[27,4,32]{2,0,1:T(8,128)}, f32[27,8,64]{2,0,1:T(8,128)})) %all-reduce.10.cloned.1.call-update) | async-done | bytes 69136 | tf_op jit(solution)/shard_map/psum | solution.py:81
  363.3 1.6 copy.94
  364.9 1.5 copy.93
  (146 shorter events, 34.7 us)
Async XLA Ops:
  7.2 181.3 %reduce-scatter.3.cloned.1.call-start = ((), (), s32[]{:S(2)}) async-start(), calls=%async_computation.2 | async-start | bytes 1114112 | tf_op jit(solution)/shard_map/reduce_scatter | solution.py:83
  8.2 12.1 %copy-start.5 = (bf16[1,32,2,8,128]{4,3,2,1,0:T(8,128)(2,1)S(1)}, bf16[1,32,2,8,128]{4,3,2,1,0:T(8,128)(2,1)}, u32[]{:S(2)}) copy-start(bf16[1,32,2,8,128]{4,3,2,1,0:T(8,128)(2,1)} %param.4) | copy-start | bytes 393220
  8.2 12.1 %collective-permute-start = (bf16[1,32,1,8,128]{4,1,3,2,0:T(8,128)(2,1)S(1)}, bf16[1,32,1,8,128]{4,1,3,2,0:T(8,128)(2,1)S(1)}, u32[]{:S(2)}, u32[]{:S(2)}) collective-permute-start(bf16[1,32,1,8,128]{4,1,3,2,0:T(8,128)(2,1)S(1)} %get-tuple-element.26), channel_id=1, source_target_pairs={{0,4},{4,8},{8,12},{1,5},{5,9},{9,13},{2,6},{6,10},{10,14},{3,7},{... | collective-permute-start | bytes 196616 | tf_op jit(solution)/shard_map/ppermute | solution.py:18
  11.7 11.3 %copy-start.7 = (bf16[27,64,32]{1,2,0:T(8,128)(2,1)S(1)}, bf16[27,64,32]{1,2,0:T(8,128)(2,1)}, u32[]{:S(2)}) copy-start(bf16[27,64,32]{1,2,0:T(8,128)(2,1)} %param.5) | copy-start | bytes 331780
  11.7 8.6 %collective-permute-start.1 = (bf16[1,32,1,8,128]{4,1,3,2,0:T(8,128)(2,1)S(1)}, bf16[1,32,1,8,128]{4,1,3,2,0:T(8,128)(2,1)S(1)}, u32[]{:S(2)}, u32[]{:S(2)}) collective-permute-start(bf16[1,32,1,8,128]{4,1,3,2,0:T(8,128)(2,1)S(1)} %get-tuple-element.25), channel_id=1, source_target_pairs={{4,0},{8,4},{12,8},{5,1},{9,5},{13,9},{6,2},{10,6},{14,10},{7,3},{... | collective-permute-start | bytes 196616 | tf_op jit(solution)/shard_map/ppermute | solution.py:19
  14.4 38.8 %collective-permute-start.8 = (bf16[1,128,1,8,128]{4,1,3,2,0:T(8,128)(2,1)S(1)}, bf16[1,128,1,8,128]{4,1,3,2,0:T(8,128)(2,1)S(1)}, u32[]{:S(2)}, u32[]{:S(2)}) collective-permute-start(bf16[1,128,1,8,128]{4,1,3,2,0:T(8,128)(2,1)S(1)} %get-tuple-element.16), channel_id=1, source_target_pairs={{0,4},{4,8},{8,12},{1,5},{5,9},{9,13},{2,6},{6,10},{10,14},{3,7},{... | collective-permute-start | bytes 786440 | tf_op jit(solution)/shard_map/ppermute | solution.py:18
  19.0 34.5 %collective-permute-start.9 = (bf16[1,128,1,8,128]{4,1,3,2,0:T(8,128)(2,1)S(1)}, bf16[1,128,1,8,128]{4,1,3,2,0:T(8,128)(2,1)S(1)}, u32[]{:S(2)}, u32[]{:S(2)}) collective-permute-start(bf16[1,128,1,8,128]{4,1,3,2,0:T(8,128)(2,1)S(1)} %get-tuple-element.15), channel_id=1, source_target_pairs={{4,0},{8,4},{12,8},{5,1},{9,5},{13,9},{6,2},{10,6},{14,10},{7,3},{... | collective-permute-start | bytes 786440 | tf_op jit(solution)/shard_map/ppermute | solution.py:19
  20.4 2.9 collective-permute-start.2
  21.7 5.6 %collective-permute-start.3 = (bf16[1,32,4,1,128]{4,1,3,2,0:T(8,128)(2,1)S(1)}, bf16[1,32,4,1,128]{4,1,3,2,0:T(8,128)(2,1)S(1)}, u32[]{:S(2)}, u32[]{:S(2)}) collective-permute-start(bf16[1,32,4,1,128]{4,1,3,2,0:T(8,128)(2,1)S(1)} %get-tuple-element.24), channel_id=1, source_target_pairs={{1,0},{2,1},{3,2},{5,4},{6,5},{7,6},{9,8},{10,9},{11,10},{13,12},{... | collective-permute-start | bytes 98312 | tf_op jit(solution)/shard_map/ppermute | solution.py:19
  34.9 6.5 %copy-start = (bf16[1,128,2,8,128]{4,3,2,1,0:T(8,128)(2,1)S(1)}, bf16[1,128,2,8,128]{4,3,2,1,0:T(8,128)(2,1)}, u32[]{:S(2)}) copy-start(bf16[1,128,2,8,128]{4,3,2,1,0:T(8,128)(2,1)} %param.7) | copy-start | bytes 1572868
  34.9 6.5 %copy-start.6 = (bf16[27,128,64]{1,2,0:T(8,128)(2,1)S(1)}, bf16[27,128,64]{1,2,0:T(8,128)(2,1)}, u32[]{:S(2)}) copy-start(bf16[27,128,64]{1,2,0:T(8,128)(2,1)} %param.6) | copy-start | bytes 1327108
  35.5 7.1 %collective-permute-start.4 = (bf16[1,64,1,8,128]{4,1,3,2,0:T(8,128)(2,1)S(1)}, bf16[1,64,1,8,128]{4,1,3,2,0:T(8,128)(2,1)S(1)}, u32[]{:S(2)}, u32[]{:S(2)}) collective-permute-start(bf16[1,64,1,8,128]{4,1,3,2,0:T(8,128)(2,1)S(1)} %get-tuple-element.21), channel_id=1, source_target_pairs={{0,4},{4,8},{8,12},{1,5},{5,9},{9,13},{2,6},{6,10},{10,14},{3,7},{... | collective-permute-start | bytes 393224 | tf_op jit(solution)/shard_map/ppermute | solution.py:18
  40.1 6.9 %collective-permute-start.5 = (bf16[1,64,1,8,128]{4,1,3,2,0:T(8,128)(2,1)S(1)}, bf16[1,64,1,8,128]{4,1,3,2,0:T(8,128)(2,1)S(1)}, u32[]{:S(2)}, u32[]{:S(2)}) collective-permute-start(bf16[1,64,1,8,128]{4,1,3,2,0:T(8,128)(2,1)S(1)} %get-tuple-element.22), channel_id=1, source_target_pairs={{4,0},{8,4},{12,8},{5,1},{9,5},{13,9},{6,2},{10,6},{14,10},{7,3},{... | collective-permute-start | bytes 393224 | tf_op jit(solution)/shard_map/ppermute | solution.py:19
  47.0 12.2 %collective-permute-start.6 = (bf16[1,64,4,1,128]{4,1,3,2,0:T(8,128)(2,1)S(1)}, bf16[1,64,4,1,128]{4,1,3,2,0:T(8,128)(2,1)S(1)}, u32[]{:S(2)}, u32[]{:S(2)}) collective-permute-start(bf16[1,64,4,1,128]{4,1,3,2,0:T(8,128)(2,1)S(1)} %get-tuple-element.19), channel_id=1, source_target_pairs={{0,1},{1,2},{2,3},{4,5},{5,6},{6,7},{8,9},{9,10},{10,11},{12,13},{... | collective-permute-start | bytes 196616 | tf_op jit(solution)/shard_map/ppermute | solution.py:18
  51.6 7.6 %collective-permute-start.7 = (bf16[1,64,4,1,128]{4,1,3,2,0:T(8,128)(2,1)S(1)}, bf16[1,64,4,1,128]{4,1,3,2,0:T(8,128)(2,1)S(1)}, u32[]{:S(2)}, u32[]{:S(2)}) collective-permute-start(bf16[1,64,4,1,128]{4,1,3,2,0:T(8,128)(2,1)S(1)} %get-tuple-element.20), channel_id=1, source_target_pairs={{1,0},{2,1},{3,2},{5,4},{6,5},{7,6},{9,8},{10,9},{11,10},{13,12},{... | collective-permute-start | bytes 196616 | tf_op jit(solution)/shard_map/ppermute | solution.py:19
  53.5 41.7 %collective-permute-start.10 = (bf16[1,128,4,1,128]{4,1,3,2,0:T(8,128)(2,1)S(1)}, bf16[1,128,4,1,128]{4,1,3,2,0:T(8,128)(2,1)S(1)}, u32[]{:S(2)}, u32[]{:S(2)}) collective-permute-start(bf16[1,128,4,1,128]{4,1,3,2,0:T(8,128)(2,1)S(1)} %get-tuple-element.13), channel_id=1, source_target_pairs={{0,1},{1,2},{2,3},{4,5},{5,6},{6,7},{8,9},{9,10},{10,11},{12,13},{... | collective-permute-start | bytes 393224 | tf_op jit(solution)/shard_map/ppermute | solution.py:18
  57.5 37.7 %collective-permute-start.11 = (bf16[1,128,4,1,128]{4,1,3,2,0:T(8,128)(2,1)S(1)}, bf16[1,128,4,1,128]{4,1,3,2,0:T(8,128)(2,1)S(1)}, u32[]{:S(2)}, u32[]{:S(2)}) collective-permute-start(bf16[1,128,4,1,128]{4,1,3,2,0:T(8,128)(2,1)S(1)} %get-tuple-element.14), channel_id=1, source_target_pairs={{1,0},{2,1},{3,2},{5,4},{6,5},{7,6},{9,8},{10,9},{11,10},{13,12},{... | collective-permute-start | bytes 393224 | tf_op jit(solution)/shard_map/ppermute | solution.py:19
  61.9 26.8 %copy-start.4 = (bf16[1,64,4,9,128]{4,1,3,2,0:T(8,128)(2,1)}, bf16[1,64,4,9,128]{4,1,3,2,0:T(8,128)(2,1)S(1)}, u32[]{:S(2)}) copy-start(bf16[1,64,4,9,128]{4,1,3,2,0:T(8,128)(2,1)S(1)} %get-tuple-element.17) | copy-start | bytes 1769476
  61.9 28.7 %copy-start.3 = (bf16[1,64,4,9,128]{4,1,3,2,0:T(8,128)(2,1)}, bf16[1,64,4,9,128]{4,1,3,2,0:T(8,128)(2,1)S(1)}, u32[]{:S(2)}) copy-start(bf16[1,64,4,9,128]{4,1,3,2,0:T(8,128)(2,1)S(1)} %get-tuple-element.18) | copy-start | bytes 1769476
  112.4 152.9 %reduce-scatter.5.cloned.1.call-start = ((), (), s32[]{:S(2)}) async-start(), calls=%async_computation.3 | async-start | bytes 2228224 | tf_op jit(solution)/shard_map/reduce_scatter | solution.py:84
  118.6 2.2 copy-start.1
  122.9 191.2 %all-reduce.8.cloned.1.call-start = ((), (), s32[]{:S(2)}) async-start(), calls=%async_computation.4 | async-start | bytes 393216 | tf_op jit(solution)/shard_map/psum | solution.py:81
  123.2 4.4 %copy-start.2 = (f32[2,8,128,128]{3,2,1,0:T(8,128)S(1)}, f32[2,8,128,128]{3,2,1,0:T(8,128)}, u32[]{:S(2)}) copy-start(f32[2,8,128,128]{3,2,1,0:T(8,128)} %convolution_add_fusion.6) | copy-start | bytes 3145732
  265.3 98.1 %all-reduce.10.cloned.1.call-start = ((), (), s32[]{:S(2)}) async-start(), calls=%async_computation.5 | async-start | bytes 393216 | tf_op jit(solution)/shard_map/psum | solution.py:81
Sparse Core Ops, SparseCore 0:
  112.5 75.8 reduce-scatter.2
  191.1 74.0 reduce-scatter.4
  268.1 45.9 all-reduce.7
  316.4 46.9 all-reduce.9
